TPU v7x, 32 devices: a whole 2x2x4 slice. The times are simulated.
32 devices in a mesh: groups: 2 (over x), seq: 16 (over z, y, core).
Axes of the slice: x: 2, y: 2, z: 4, core: 2. Of those that a mesh axis runs over, the one named last changes fastest.
Arguments:
- queries: bfloat16 [64, 4, 8192], P(('groups', 'seq')), parts along dimension 0, may hold values from -128 to 128
- step_keys: bfloat16 [64, 4, 1024], P(('groups', 'seq')), parts along dimension 0, may hold values from -15 to 15
- step_values: bfloat16 [64, 4, 1024], P(('groups', 'seq')), parts along dimension 0, may hold values from -48 to 48
- sample_keys: bfloat16 [64, 1024, 1024], P(('groups', 'seq')), parts along dimension 0, may hold values from -6 to 6
- sample_values: bfloat16 [64, 1024, 1024], P(('groups', 'seq')), parts along dimension 0, may hold values from -48 to 48
- suffix_len: int32 [64], P(('groups', 'seq')), parts along dimension 0, may hold values from 128 to 1024
- prompt_id: int32 [64], P(('groups', 'seq')), parts along dimension 0, may hold values from 0 to 1, as said below
- document_keys: bfloat16 [4, 4096, 1024], P('groups', 'seq'), parts along dimension 0, may hold values from -6 to 6
- document_values: bfloat16 [4, 4096, 1024], P('groups', 'seq'), parts along dimension 0, may hold values from -48 to 48
Outputs:
- attended: bfloat16 [64, 4, 8192], P(('groups', 'seq')), parts along dimension 0
There are 2 independent parts, one for each index of `groups`. A program takes and returns all parts, laid end to end along the dimension named above; each array names one. Nothing has to cross between parts.
Inputs may be any that keep to these rules, and one draw needn't show every extreme that they name: `prompt_id`: each prompt id is held by exactly 16 samples.
All inputs are finite; a program needn't handle non-finite values.
Results may differ from a plain program's by a relative error of at most 0.0013.
Values may be sent and summed in bfloat16 or wider, within the bound.
No kernel may reach another device: no remote copies, remote signals or barrier semaphores. Data moves between devices by JAX's collectives and lax.ppermute only.
A program may use at most 192 MiB of HBM per device.

v0:
```python
import functools
import math

import jax
import jax.numpy as jnp
from jax import lax
from jax.experimental import pallas as pl
from jax.experimental.pallas import tpu as pltpu
from jax.sharding import PartitionSpec as P


QUERY_HEADS = 64
KEY_VALUE_HEADS = 8
HEAD_SIZE = 128
GROUP = QUERY_HEADS // KEY_VALUE_HEADS
SCALING = HEAD_SIZE ** (-0.5)
LANES = 128
FIRST = (6,)
EARLY = (7, 2)
LATE = (4, 5, 3, 1)
LIMIT = pltpu.CompilerParams(vmem_limit_bytes=24 * 1024 * 1024)
LEVELS = 32767.0
CODE_STEPS = 256.0
REST_STEPS = 65000.0
TINY = 2.0**-100
AUX_ROWS = 8
LOAD_PARTS = 4
WEIGHT_SCALE = SCALING * math.log2(math.e)


def whole(space=pltpu.VMEM):
    return pl.BlockSpec(memory_space=space)


def near(array):
    return pltpu.with_memory_space_constraint(array, pltpu.VMEM)


def far(array):
    return pltpu.with_memory_space_constraint(array, pltpu.HBM)


def start_slices(partners, keys_ref, values_ref, out_refs, sem):
    mine = lax.axis_index("seq") % KEY_VALUE_HEADS
    copies = []
    for slot, partner in enumerate(partners):
        head = jnp.bitwise_xor(mine, partner)
        columns = pl.ds(pl.multiple_of(head * HEAD_SIZE, HEAD_SIZE), HEAD_SIZE)
        for side, source in enumerate((keys_ref, values_ref)):
            copy = pltpu.make_async_copy(
                source.at[:, :, columns], out_refs[slot].at[side], sem.at[slot, side]
            )
            copy.start()
            copies.append(copy)
    return copies


def slice_kernel(partners, keys_ref, values_ref, *refs):
    for copy in start_slices(partners, keys_ref, values_ref, refs[:-1], refs[-1]):
        copy.wait()


def head_slices(keys, values, partners):
    prompts, block, _ = keys.shape
    piece = jax.ShapeDtypeStruct((2, prompts, block, HEAD_SIZE), keys.dtype)
    pieces = pl.pallas_call(
        functools.partial(slice_kernel, partners),
        out_shape=[piece] * len(partners),
        in_specs=[whole(pltpu.HBM)] * 2,
        out_specs=[whole()] * len(partners),
        scratch_shapes=[pltpu.SemaphoreType.DMA((len(partners), 2))],
        compiler_params=LIMIT,
        name="head_slices",
    )(far(keys), far(values))
    return pieces


def pack_rows(ids_ref, queries_ref, out_ref):
    owned, steps, _ = queries_ref.shape
    rows = owned * steps * GROUP
    lane = lax.broadcasted_iota(jnp.int32, (out_ref.shape[1] - rows, LANES), 1)
    marks = jnp.zeros(lane.shape, jnp.float32)
    for n in range(owned):
        marks = jnp.where(lane == n, ids_ref[n].astype(jnp.float32), marks)
    marks = marks.astype(jnp.bfloat16)
    for head in range(KEY_VALUE_HEADS):
        parts = []
        for n in range(owned):
            for r in range(GROUP):
                first = (head * GROUP + r) * HEAD_SIZE
                parts.append(queries_ref[n, :, first : first + HEAD_SIZE].astype(jnp.float32))
        block = jnp.concatenate(parts, axis=0).astype(jnp.bfloat16)
        for copy in range(out_ref.shape[0] // KEY_VALUE_HEADS):
            out_ref[copy * KEY_VALUE_HEADS + head, :rows, :] = block
            out_ref[copy * KEY_VALUE_HEADS + head, rows:, :] = marks


def slice_and_pack_kernel(partners, keys_ref, values_ref, ids_ref, queries_ref, *refs):
    out_refs, packed_ref, query_buffer, sem, query_sem = refs[:-4], *refs[-4:]
    load = pltpu.make_async_copy(queries_ref, query_buffer, query_sem)
    load.start()
    copies = start_slices(partners, keys_ref, values_ref, out_refs, sem)
    load.wait()
    pack_rows(ids_ref, query_buffer, packed_ref)
    for copy in copies:
        copy.wait()


def slices_and_queries(keys, values, partners, queries, prompt_id, devices):
    prompts, block, _ = keys.shape
    owned, steps, _ = queries.shape
    piece = jax.ShapeDtypeStruct((2, prompts, block, HEAD_SIZE), keys.dtype)
    rows = owned * steps * GROUP + AUX_ROWS
    results = pl.pallas_call(
        functools.partial(slice_and_pack_kernel, partners),
        out_shape=[piece] * len(partners)
        + [jax.ShapeDtypeStruct((devices, rows, HEAD_SIZE), jnp.bfloat16)],
        in_specs=[whole(pltpu.HBM)] * 2 + [whole(pltpu.SMEM), whole(pltpu.HBM)],
        out_specs=[whole()] * (len(partners) + 1),
        scratch_shapes=[
            pltpu.VMEM(queries.shape, queries.dtype),
            pltpu.SemaphoreType.DMA((len(partners), 2)),
            pltpu.SemaphoreType.DMA,
        ],
        compiler_params=LIMIT,
        name="slices_and_queries",
    )(far(keys), far(values), far(prompt_id), far(queries))
    return results[:-1], results[-1]


def contract(left, right, dims):
    return lax.dot_general(left, right, (dims, ((), ())), preferred_element_type=jnp.float32)


def diagonal(rows, shift=0):
    row = lax.broadcasted_iota(jnp.int32, (rows, LANES), 0) + shift
    lane = lax.broadcasted_iota(jnp.int32, (rows, LANES), 1)
    return (lane == row) | (lane == row + LANES // 2)


def diagonal_row(columns, mask):
    return jnp.sum(jnp.where(mask, columns, 0.0), axis=0, keepdims=True)


def left_right(left, right):
    lane = lax.broadcasted_iota(jnp.int32, (left.shape[0], LANES), 1)
    return jnp.where(lane < LANES // 2, left, right)


def to_words(values):
    return jnp.round(values).astype(jnp.int32).astype(jnp.int16)


def from_words(words):
    return words.astype(jnp.int32).astype(jnp.float32)


def suffix_kernel(
    len_ref, query_ref, keys_hbm, values_hbm, new_keys_ref, new_values_ref, out_ref, aux_ref, keys_ref, values_ref, sem
):
    owned, slots, _ = keys_ref.shape
    steps = new_keys_ref.shape[1]
    rows = steps * GROUP
    loads = {}
    for n in range(owned):
        for side, (source, target) in enumerate(((keys_hbm, keys_ref), (values_hbm, values_ref))):
            for part in range(LOAD_PARTS):
                span = pl.ds(part * (slots // LOAD_PARTS), slots // LOAD_PARTS)
                load = pltpu.make_async_copy(
                    source.at[n, span], target.at[n, span], sem.at[n, side, part]
                )
                load.start()
                loads.setdefault((n, side), []).append(load)
    aux = [None] * KEY_VALUE_HEADS
    for n in range(owned):
        mask = diagonal(rows, n * rows)
        for load in loads[n, 0]:
            load.wait()
        scores = []
        for h in range(KEY_VALUE_HEADS):
            columns = slice(h * HEAD_SIZE, (h + 1) * HEAD_SIZE)
            query = query_ref[h, n * rows : (n + 1) * rows, :]
            cache = contract(query, keys_ref[n, :, columns], ((1,), (1,))) * SCALING
            fresh = contract(query, new_keys_ref[n, :, columns], ((1,), (1,))) * SCALING
            cache_live = lax.broadcasted_iota(jnp.int32, cache.shape, 1) < len_ref[n]
            fresh_live = (
                lax.broadcasted_iota(jnp.int32, fresh.shape, 1)
                <= lax.broadcasted_iota(jnp.int32, fresh.shape, 0) % steps
            )
            peak = jnp.maximum(
                jnp.max(jnp.where(cache_live, cache, -jnp.inf), axis=1, keepdims=True),
                jnp.max(jnp.where(fresh_live, fresh, -jnp.inf), axis=1, keepdims=True),
            )
            cache_exp = jnp.where(cache_live, jnp.exp(cache - peak), 0.0)
            fresh_exp = jnp.where(fresh_live, jnp.exp(fresh - peak), 0.0)
            total = jnp.sum(cache_exp, axis=1, keepdims=True) + jnp.sum(
                fresh_exp, axis=1, keepdims=True
            )
            row = diagonal_row(left_right(peak, total), mask)
            aux[h] = row if aux[h] is None else aux[h] + row
            scores.append((cache_exp.astype(jnp.bfloat16), fresh_exp.astype(jnp.bfloat16)))
        for load in loads[n, 1]:
            load.wait()
        for h in range(KEY_VALUE_HEADS):
            columns = slice(h * HEAD_SIZE, (h + 1) * HEAD_SIZE)
            cache_exp, fresh_exp = scores[h]
            out_ref[h, n * rows : (n + 1) * rows, :] = contract(
                cache_exp, values_ref[n, :, columns], ((1,), (0,))
            ) + contract(fresh_exp, new_values_ref[n, :, columns], ((1,), (0,)))
    for h in range(KEY_VALUE_HEADS):
        aux_ref[h] = aux[h]


def suffix_part(suffix_len, packed, keys, values, new_keys, new_values):
    owned, _, _ = keys.shape
    rows = owned * new_keys.shape[1] * GROUP
    return pl.pallas_call(
        suffix_kernel,
        out_shape=[
            jax.ShapeDtypeStruct((KEY_VALUE_HEADS, rows, HEAD_SIZE), jnp.float32),
            jax.ShapeDtypeStruct((KEY_VALUE_HEADS, 1, LANES), jnp.float32),
        ],
        in_specs=[whole(pltpu.SMEM), whole()]
        + [whole(pltpu.HBM)] * 2
        + [whole()] * 2,
        out_specs=[whole()] * 2,
        scratch_shapes=[
            pltpu.VMEM(keys.shape, keys.dtype),
            pltpu.VMEM(values.shape, values.dtype),
            pltpu.SemaphoreType.DMA((owned, 2, LOAD_PARTS)),
        ],
        compiler_params=LIMIT,
        name="suffix_part",
    )(suffix_len, packed, keys, values, new_keys, new_values)


def attend(query, pieces, prompt, state):
    scores = [contract(query, piece[0, prompt], ((1,), (1,))) for piece in pieces]
    peaks = [jnp.max(score, axis=1, keepdims=True) for score in scores]
    weights = [jnp.exp2((score - peak) * WEIGHT_SCALE) for score, peak in zip(scores, peaks)]
    parts = [
        contract(weight.astype(jnp.bfloat16), piece[1, prompt], ((1,), (0,)))
        for weight, piece in zip(weights, pieces)
    ]
    totals = [jnp.sum(weight, axis=1, keepdims=True) for weight in weights]
    shape = parts[0].shape
    tops = [jnp.broadcast_to(peak * SCALING, shape) for peak in peaks]
    masses = [jnp.broadcast_to(total, shape) for total in totals]
    if state is not None:
        tops.append(state[0])
        masses.append(state[1])
        parts.append(state[2])
    top = functools.reduce(jnp.maximum, tops)
    factors = [jnp.exp(t - top) for t in tops]
    mass = functools.reduce(jnp.add, [m * f for m, f in zip(masses, factors)])
    out = functools.reduce(jnp.add, [p * f for p, f in zip(parts, factors)])
    return top, mass, out


def find_places(ids, prompts, rows):
    samples = ids.shape[0]
    order = jnp.arange(samples, dtype=jnp.int32)
    earlier = (ids[None, :] == ids[:, None]) & (order[None, :] < order[:, None])
    rank = jnp.sum(earlier.astype(jnp.int32), axis=1)
    return (ids * (samples // prompts) + rank) * rows


def first_kernel(rows, chunk, place_ref, queries_ref, *refs):
    pieces, refs = refs[:-4], refs[-4:]
    sorted_ref, out_ref, peak_ref, total_ref = refs
    devices = queries_ref.shape[0]
    owned = place_ref.shape[0] // devices
    prompts = pieces[0].shape[1]

    def sort_one(device, carry):
        for n in range(owned):
            target = pl.ds(pl.multiple_of(place_ref[device * owned + n], rows), rows)
            sorted_ref[target, :] = queries_ref[device, n * rows : (n + 1) * rows, :]
        return carry

    lax.fori_loop(0, devices, sort_one, 0, unroll=4)
    chunks = sorted_ref.shape[0] // prompts // chunk

    def step(index, carry):
        target = pl.ds(pl.multiple_of(index * chunk, chunk), chunk)
        peak, total, out = attend(sorted_ref[target, :], pieces, index // chunks, None)
        out_ref[target, :] = out
        peak_ref[target, :] = peak
        total_ref[target, :] = total
        return carry

    lax.fori_loop(0, prompts * chunks, step, 0, unroll=2)


def next_kernel(chunk, sorted_ref, acc_in, peak_in, total_in, *refs):
    pieces, (acc_ref, peak_ref, total_ref) = refs[:-3], refs[-3:]
    prompts = pieces[0].shape[1]
    chunks = sorted_ref.shape[0] // prompts // chunk

    def step(index, carry):
        target = pl.ds(pl.multiple_of(index * chunk, chunk), chunk)
        state = (peak_in[target, :], total_in[target, :], acc_in[target, :])
        peak, total, out = attend(sorted_ref[target, :], pieces, index // chunks, state)
        acc_ref[target, :] = out
        peak_ref[target, :] = peak
        total_ref[target, :] = total
        return carry

    lax.fori_loop(0, prompts * chunks, step, 0, unroll=2)


def last_kernel(rows, chunk, place_ref, sorted_ref, acc_ref, peak_ref, total_ref, *refs):
    pieces, refs = refs[:-3], refs[-3:]
    out_ref, out_scratch, aux_scratch = refs
    devices = out_ref.shape[0]
    owned = place_ref.shape[0] // devices
    prompts = pieces[0].shape[1]
    chunks = sorted_ref.shape[0] // prompts // chunk

    def step(index, carry):
        target = pl.ds(pl.multiple_of(index * chunk, chunk), chunk)
        state = (peak_ref[target, :], total_ref[target, :], acc_ref[target, :])
        peak, total, out = attend(sorted_ref[target, :], pieces, index // chunks, state)
        out = out / total
        largest = jnp.max(jnp.abs(out), axis=1, keepdims=True)
        code = jnp.ceil(jnp.log2(jnp.maximum(largest, TINY)) * CODE_STEPS)
        out = out * (LEVELS * jnp.exp2(code * (-1.0 / CODE_STEPS)))
        out_scratch[target, :] = to_words(jnp.clip(out, -LEVELS, LEVELS))
        aux_scratch[target, :] = left_right(peak + jnp.log(total), code)
        return carry

    lax.fori_loop(0, prompts * chunks, step, 0, unroll=2)

    mask = diagonal(owned * rows)
    first_rows = lax.broadcasted_iota(jnp.int32, (AUX_ROWS, LANES), 0) < AUX_ROWS // 2

    def emit(device, carry):
        aux_parts = []
        for n in range(owned):
            source = pl.ds(pl.multiple_of(place_ref[device * owned + n], rows), rows)
            out_ref[device, n * rows : (n + 1) * rows, :] = out_scratch[source, :]
            aux_parts.append(aux_scratch[source, :])
        row = diagonal_row(jnp.concatenate(aux_parts, axis=0), mask)
        near_part = jnp.round(row)
        rest = (row - near_part) * REST_STEPS
        words = jnp.where(first_rows, near_part, rest)
        out_ref[device, owned * rows :, :] = to_words(words)
        return carry

    lax.fori_loop(0, devices, emit, 0, unroll=4)


def first_stage(places, queries, pieces, rows):
    prompts = pieces[0].shape[1]
    total = places.shape[0] * rows
    results = pl.pallas_call(
        functools.partial(first_kernel, rows, min(512, total // prompts)),
        out_shape=[
            jax.ShapeDtypeStruct((total, HEAD_SIZE), jnp.bfloat16),
            jax.ShapeDtypeStruct((total, HEAD_SIZE), jnp.float32),
            jax.ShapeDtypeStruct((total, LANES), jnp.float32),
            jax.ShapeDtypeStruct((total, LANES), jnp.float32),
        ],
        in_specs=[whole(pltpu.SMEM)] + [whole()] * (1 + len(pieces)),
        out_specs=[whole()] * 4,
        compiler_params=LIMIT,
        name="first_stage",
    )(places, queries, *pieces)
    return [near(result) for result in results]


def next_stage(state, pieces):
    total = state[0].shape[0]
    prompts = pieces[0].shape[1]
    results = pl.pallas_call(
        functools.partial(next_kernel, min(512, total // prompts)),
        out_shape=[jax.ShapeDtypeStruct((total, HEAD_SIZE), jnp.float32)] * 3,
        in_specs=[whole()] * (4 + len(pieces)),
        out_specs=[whole()] * 3,
        compiler_params=LIMIT,
        name="next_stage",
    )(*state, *pieces)
    return [state[0]] + [near(result) for result in results]


def last_stage(places, state, pieces, rows, devices):
    prompts = pieces[0].shape[1]
    total = places.shape[0] * rows
    return pl.pallas_call(
        functools.partial(last_kernel, rows, min(512, total // prompts)),
        out_shape=jax.ShapeDtypeStruct((devices, total // devices + AUX_ROWS, HEAD_SIZE), jnp.int16),
        in_specs=[whole(pltpu.SMEM)] + [whole()] * (4 + len(pieces)),
        out_specs=whole(),
        scratch_shapes=[
            pltpu.VMEM((total, HEAD_SIZE), jnp.int16),
            pltpu.VMEM((total, HEAD_SIZE), jnp.float32),
        ],
        compiler_params=LIMIT,
        name="last_stage",
    )(places, *state, *pieces)


def merge_kernel(got_ref, local_ref, local_aux_ref, out_ref):
    owned, steps, _ = out_ref.shape
    rows = local_ref.shape[1]
    half = LANES // 2
    groups = got_ref.shape[0] // KEY_VALUE_HEADS
    local_aux = local_aux_ref[:, 0, :]
    local_total = local_aux[:, half:]
    levels = [local_aux[:, :half] + jnp.log(local_total)]
    scales = [1.0 / local_total]
    for g in range(groups):
        both = []
        for h in range(KEY_VALUE_HEADS):
            words = from_words(got_ref[g * KEY_VALUE_HEADS + h, rows:, :])
            middle = AUX_ROWS // 2
            both.append(words[:1] + words[middle : middle + 1] * (1.0 / REST_STEPS))
        aux = jnp.concatenate(both, axis=0)
        levels.append(aux[:, :half])
        scales.append(jnp.exp2(aux[:, half:] * (1.0 / CODE_STEPS)) * (1.0 / LEVELS))
    highest = functools.reduce(jnp.maximum, levels)
    weights = [jnp.exp(level - highest) for level in levels]
    denominator = functools.reduce(jnp.add, weights)
    factors = [jnp.transpose(w * s / denominator) for w, s in zip(weights, scales)]
    for h in range(KEY_VALUE_HEADS):
        result = local_ref[h] * factors[0][:, h : h + 1]
        for g in range(groups):
            part = from_words(got_ref[g * KEY_VALUE_HEADS + h, :rows, :])
            result += part * factors[g + 1][:, h : h + 1]
        for n in range(owned):
            for r in range(GROUP):
                first = (h * GROUP + r) * HEAD_SIZE
                start = (n * GROUP + r) * steps
                out_ref[n, :, first : first + HEAD_SIZE] = result[start : start + steps, :].astype(
                    jnp.bfloat16
                )


def merge(got, local, local_aux, shape):
    return pl.pallas_call(
        merge_kernel,
        out_shape=jax.ShapeDtypeStruct(shape, jnp.bfloat16),
        in_specs=[whole()] * 3,
        out_specs=whole(),
        compiler_params=LIMIT,
        name="merge",
    )(got, local, local_aux)


def body(
    queries,
    step_keys,
    step_values,
    sample_keys,
    sample_values,
    suffix_len,
    prompt_id,
    document_keys,
    document_values,
):
    owned, steps, _ = queries.shape
    devices = lax.axis_size("seq")
    rows = steps * GROUP
    assert 2 * owned * rows == LANES and devices % KEY_VALUE_HEADS == 0
    arrived = {}

    def exchange(piece, partner):
        route = [(i, i ^ partner) for i in range(devices)]
        arrived[partner] = near(lax.ppermute(piece, "seq", route))

    slices = head_slices(document_keys, document_values, FIRST)
    exchange(slices[0], FIRST[0])
    slices, packed = slices_and_queries(
        document_keys, document_values, EARLY, queries, prompt_id, devices
    )
    for partner, piece in zip(EARLY, slices):
        exchange(piece, partner)
    head_queries = lax.all_to_all(packed, "seq", split_axis=0, concat_axis=0, tiled=True)
    slices = head_slices(document_keys, document_values, LATE + (0,))
    arrived[0] = near(slices[-1])
    for partner, piece in zip(LATE, slices):
        exchange(piece, partner)
    head_ids = head_queries[:, owned * rows, :owned].reshape(-1).astype(jnp.int32)
    places = find_places(head_ids, document_keys.shape[0], rows)
    ready = [arrived[k] for k in (0, 6, 7, 1, 4, 2)]
    state = first_stage(places, near(head_queries), ready, rows)
    state = next_stage(state, [arrived[3]])
    sent = last_stage(places, state, [arrived[5]], rows, devices)
    local, local_aux = suffix_part(
        suffix_len, packed, far(sample_keys), far(sample_values), step_keys, step_values
    )
    got = near(lax.all_to_all(sent, "seq", split_axis=0, concat_axis=0, tiled=True))
    return merge(got, near(local), near(local_aux), queries.shape)


def solution(mesh):
    shared = P(("groups", "seq"), None, None)
    split = P("groups", "seq", None)
    return jax.shard_map(
        body,
        mesh=mesh,
        in_specs=(shared,) * 5 + (P(("groups", "seq")),) * 2 + (split,) * 2,
        out_specs=shared,
        check_vma=False,
    )
```

profile of v0, /device:TPU:0, one launch (start us, length us, event | category | flops | bytes accessed | tf_op | source)
XLA Modules:
  0.0 59.6 jit_solution(22711351805166567)
XLA Ops:
  0.0 2.6 %slices_and_queries.1 = (bf16[2,2,256,128]{3,2,1,0:T(8,128)(2,1)S(1)}, bf16[2,2,256,128]{3,2,1,0:T(8,128)(2,1)S(1)}, bf16[16,72,128]{2,1,0:T(8,128)(2,1)}) custom-call(bf16[2,256,1024]{2,1,0:T(8,128)(2,1)} %keys_ref.5, bf16[2,256,1024]{2,1,0:T(8,128)(2,1)} %values_ref.5, s32[2]{0:T(128)} %ids_ref.1, bf16[2,4,8192]{2,1,0:T(4,128)(2,1)} %queries_ref.1), custom_call_target="tpu_custom_call" | custom-call | tf_op jit(solution)/shard_map/slices_and_queries/pallas_call | solution.py:114
  2.6 7.4 %all-to-all-start = ((bf16[16,72,128]{2,1,0:T(8,128)(2,1)}), bf16[16,72,128]{2,1,0:T(8,128)(2,1)S(1)}, u32[]{:S(2)}, u32[]{:S(2)}) async-start(bf16[16,72,128]{2,1,0:T(8,128)(2,1)} %get-tuple-element.22.query_ref), calls=%async_computation | async-start | bytes 589824 | tf_op jit(solution)/shard_map/all_to_all | solution.py:478
  10.0 1.0 %head_slices.3 = bf16[2,2,256,128]{3,2,1,0:T(8,128)(2,1)S(1)} custom-call(bf16[2,256,1024]{2,1,0:T(8,128)(2,1)} %keys_ref.5, bf16[2,256,1024]{2,1,0:T(8,128)(2,1)} %values_ref.5), custom_call_target="tpu_custom_call" | custom-call | tf_op jit(solution)/shard_map/head_slices/pallas_call | solution.py:66
  11.0 2.9 %collective-permute-start = (bf16[2,2,256,128]{3,2,1,0:T(8,128)(2,1)S(1)}, bf16[2,2,256,128]{3,2,1,0:T(8,128)(2,1)S(1)}, u32[]{:S(2)}, u32[]{:S(2)}) collective-permute-start(bf16[2,2,256,128]{3,2,1,0:T(8,128)(2,1)S(1)} %head_slices.3), channel_id=1, source_target_pairs={{0,6},{1,7},{2,4},{3,5},{4,2},{5,3},{6,0},{7,1},{8,14},{9,15},{10,... | collective-permute-start | bytes 786440 | tf_op jit(solution)/shard_map/ppermute | solution.py:469
  13.9 0.0 collective-permute-start.1
  13.9 0.0 copy-start.1
  13.9 1.5 %collective-permute-start.4 = (bf16[2,2,256,128]{3,2,1,0:T(8,128)(2,1)S(1)}, bf16[2,2,256,128]{3,2,1,0:T(8,128)(2,1)S(1)}, u32[]{:S(2)}, u32[]{:S(2)}) collective-permute-start(bf16[2,2,256,128]{3,2,1,0:T(8,128)(2,1)S(1)} %get-tuple-element.27), channel_id=1, source_target_pairs={{0,2},{1,3},{2,0},{3,1},{4,6},{5,7},{6,4},{7,5},{8,10},{9,11},{10,... | collective-permute-start | bytes 786440 | tf_op jit(solution)/shard_map/ppermute | solution.py:469
  15.4 2.2 %head_slices.2 = (bf16[2,2,256,128]{3,2,1,0:T(8,128)(2,1)S(1)}, bf16[2,2,256,128]{3,2,1,0:T(8,128)(2,1)S(1)}, bf16[2,2,256,128]{3,2,1,0:T(8,128)(2,1)S(1)}, bf16...) custom-call(bf16[2,256,1024]{2,1,0:T(8,128)(2,1)} %keys_ref.5, bf16[2,256,1024]{2,1,0:T(8,128)(2,1)} %values_ref.5), custom_call_target="tpu_custom_call" | custom-call | tf_op jit(solution)/shard_map/head_slices/pallas_call | solution.py:66
  17.6 0.5 collective-permute-start.2
  18.0 1.5 %collective-permute-start.3 = (bf16[2,2,256,128]{3,2,1,0:T(8,128)(2,1)S(1)}, bf16[2,2,256,128]{3,2,1,0:T(8,128)(2,1)S(1)}, u32[]{:S(2)}, u32[]{:S(2)}) collective-permute-start(bf16[2,2,256,128]{3,2,1,0:T(8,128)(2,1)S(1)} %get-tuple-element.26), channel_id=1, source_target_pairs={{0,4},{1,5},{2,6},{3,7},{4,0},{5,1},{6,2},{7,3},{8,12},{9,13},{10,... | collective-permute-start | bytes 786440 | tf_op jit(solution)/shard_map/ppermute | solution.py:469
  19.5 1.6 %all-to-all-done.queries_ref = bf16[16,72,128]{2,1,0:T(8,128)(2,1)S(1)} async-done(((bf16[16,72,128]{2,1,0:T(8,128)(2,1)}), bf16[16,72,128]{2,1,0:T(8,128)(2,1)S(1)}, u32[]{:S(2)}, u32[]{:S(2)}) %all-to-all-start) | async-done | bytes 294944 | tf_op jit(solution)/shard_map/all_to_all | solution.py:478
  21.2 0.1 reshape.12
  21.3 3.7 %collective-permute-done.refs_1_ = bf16[2,2,256,128]{3,2,1,0:T(8,128)(2,1)S(1)} collective-permute-done((bf16[2,2,256,128]{3,2,1,0:T(8,128)(2,1)S(1)}, bf16[2,2,256,128]{3,2,1,0:T(8,128)(2,1)S(1)}, u32[]{:S(2)}, u32[]{:S(2)}) %collective-permute-start) | collective-permute-done | bytes 262176 | tf_op jit(solution)/shard_map/ppermute | solution.py:469
  25.0 0.0 collective-permute-start.5
  25.0 4.5 %collective-permute-done.1.refs_2_ = bf16[2,2,256,128]{3,2,1,0:T(8,128)(2,1)S(1)} collective-permute-done((bf16[2,2,256,128]{3,2,1,0:T(8,128)(2,1)S(1)}, bf16[2,2,256,128]{3,2,1,0:T(8,128)(2,1)S(1)}, u32[]{:S(2)}, u32[]{:S(2)}) %collective-permute-start.1) | collective-permute-done | bytes 262176 | tf_op jit(solution)/shard_map/ppermute | solution.py:469
  29.4 1.7 %collective-permute-start.6 = (bf16[2,2,256,128]{3,2,1,0:T(8,128)(2,1)S(1)}, bf16[2,2,256,128]{3,2,1,0:T(8,128)(2,1)S(1)}, u32[]{:S(2)}, u32[]{:S(2)}) collective-permute-start(bf16[2,2,256,128]{3,2,1,0:T(8,128)(2,1)S(1)} %get-tuple-element.36), channel_id=1, source_target_pairs={{0,5},{1,4},{2,7},{3,6},{4,1},{5,0},{6,3},{7,2},{8,13},{9,12},{10,... | collective-permute-start | bytes 786440 | tf_op jit(solution)/shard_map/ppermute | solution.py:469
  31.1 0.2 convert_reduce_fusion
  31.3 3.5 %collective-permute-done.4.refs_5_ = bf16[2,2,256,128]{3,2,1,0:T(8,128)(2,1)S(1)} collective-permute-done((bf16[2,2,256,128]{3,2,1,0:T(8,128)(2,1)S(1)}, bf16[2,2,256,128]{3,2,1,0:T(8,128)(2,1)S(1)}, u32[]{:S(2)}, u32[]{:S(2)}) %collective-permute-start.4) | collective-permute-done | bytes 262176 | tf_op jit(solution)/shard_map/ppermute | solution.py:469
  34.8 0.0 collective-permute-done.2.refs_3_
  34.8 0.2 collective-permute-done.3.refs_4_
  35.0 3.7 %first_stage.1 = (bf16[1024,128]{1,0:T(8,128)(2,1)S(1)}, f32[1024,128]{1,0:T(8,128)S(1)}, f32[1024,128]{1,0:T(8,128)S(1)}, f32[1024,128]{1,0:T(8,128)S(1)}) custom-call(s32[32]{0:T(128)S(1)} %add_multiply_fusion.place_ref, bf16[16,72,128]{2,1,0:T(8,128)(2,1)S(1)} %all-to-all-done.queries_ref, bf16[2,2,256,128]{3,2,1,0:T(8,128)(2,1)S(1)} %get-tuple-element.23.refs_0_, ...), custom_call_target="tpu_custom_call" | custom-call | tf_op jit(solution)/shard_map/first_stage/pallas_call | solution.py:356
  38.7 1.2 %collective-permute-done.5.refs_0_ = bf16[2,2,256,128]{3,2,1,0:T(8,128)(2,1)S(1)} collective-permute-done((bf16[2,2,256,128]{3,2,1,0:T(8,128)(2,1)S(1)}, bf16[2,2,256,128]{3,2,1,0:T(8,128)(2,1)S(1)}, u32[]{:S(2)}, u32[]{:S(2)}) %collective-permute-start.5) | collective-permute-done | bytes 262176 | tf_op jit(solution)/shard_map/ppermute | solution.py:469
  39.9 0.8 %next_stage.1 = (f32[1024,128]{1,0:T(8,128)S(1)}, f32[1024,128]{1,0:T(8,128)S(1)}, f32[1024,128]{1,0:T(8,128)S(1)}) custom-call(bf16[1024,128]{1,0:T(8,128)(2,1)S(1)} %get-tuple-element.28.sorted_ref, f32[1024,128]{1,0:T(8,128)S(1)} %get-tuple-element.29.acc_in, f32[1024,128]{1,0:T(8,128)S(1)} %get-tuple-element.30.peak_in, ...), custom_call_target="tpu_custom_call" | custom-call | tf_op jit(solution)/shard_map/next_stage/pallas_call | solution.py:375
  40.7 0.0 collective-permute-done.6.refs_0_
  40.7 2.4 %last_stage.1 = s16[16,72,128]{2,1,0:T(8,128)(2,1)} custom-call(s32[32]{0:T(128)S(1)} %add_multiply_fusion.place_ref, bf16[1024,128]{1,0:T(8,128)(2,1)S(1)} %get-tuple-element.28.sorted_ref, f32[1024,128]{1,0:T(8,128)S(1)} %get-tuple-element.33.acc_ref, f32[1024,128]{1,0:T(8,128)S(1)} %get-tuple-element.34.peak_ref, ...), custom_call_target="tpu_custom_call" | custom-call | tf_op jit(solution)/shard_map/last_stage/pallas_call | solution.py:389
  43.1 4.8 %all-to-all-start.1 = ((s16[16,72,128]{2,1,0:T(8,128)(2,1)}), s16[16,72,128]{2,1,0:T(8,128)(2,1)S(1)}, u32[]{:S(2)}, u32[]{:S(2)}) async-start(s16[16,72,128]{2,1,0:T(8,128)(2,1)} %last_stage.1), calls=%async_computation.1 | async-start | bytes 589824 | tf_op jit(solution)/shard_map/all_to_all | solution.py:492
  47.9 0.0 copy-done
  47.9 0.0 copy-done.1
  47.9 0.0 copy-done.2
  47.9 6.2 %suffix_part.1 = (f32[8,64,128]{2,1,0:T(8,128)S(1)}, f32[8,1,128]{2,1,0:T(1,128)S(1)}) custom-call(s32[2]{0:T(128)S(1)} %copy-done.2, bf16[16,72,128]{2,1,0:T(8,128)(2,1)} %get-tuple-element.22.query_ref, bf16[2,1024,1024]{2,1,0:T(8,128)(2,1)} %keys_hbm.1, bf16[2,1024,1024]{2,1,0:T(8,128)(2,1)} %values_hbm.1, bf16[2,4,1024]{2,1,0:T(4,128)(2,1)S(1)} %copy-done, ...), custom_call_target="tpu_custom_call" | custom-call | tf_op jit(solution)/shard_map/suffix_part/pallas_call | solution.py:217
  54.1 4.3 %all-to-all-done.1.got_ref = s16[16,72,128]{2,1,0:T(8,128)(2,1)S(1)} async-done(((s16[16,72,128]{2,1,0:T(8,128)(2,1)}), s16[16,72,128]{2,1,0:T(8,128)(2,1)S(1)}, u32[]{:S(2)}, u32[]{:S(2)}) %all-to-all-start.1) | async-done | bytes 294944 | tf_op jit(solution)/shard_map/all_to_all | solution.py:492
  58.4 1.1 %merge.1 = bf16[2,4,8192]{2,1,0:T(4,128)(2,1)} custom-call(s16[16,72,128]{2,1,0:T(8,128)(2,1)S(1)} %all-to-all-done.1.got_ref, f32[8,64,128]{2,1,0:T(8,128)S(1)} %get-tuple-element.37.local_ref, f32[8,1,128]{2,1,0:T(1,128)S(1)} %get-tuple-element.38.local_aux_ref), custom_call_target="tpu_custom_call" | custom-call | tf_op jit(solution)/shard_map/merge/pallas_call | solution.py:440
  (4 shorter events, 0.0 us)
Async XLA Ops:
  2.6 18.6 %all-to-all-start = ((bf16[16,72,128]{2,1,0:T(8,128)(2,1)}), bf16[16,72,128]{2,1,0:T(8,128)(2,1)S(1)}, u32[]{:S(2)}, u32[]{:S(2)}) async-start(bf16[16,72,128]{2,1,0:T(8,128)(2,1)} %get-tuple-element.22.query_ref), calls=%async_computation | async-start | bytes 589824 | tf_op jit(solution)/shard_map/all_to_all | solution.py:478
  11.0 13.9 %collective-permute-start = (bf16[2,2,256,128]{3,2,1,0:T(8,128)(2,1)S(1)}, bf16[2,2,256,128]{3,2,1,0:T(8,128)(2,1)S(1)}, u32[]{:S(2)}, u32[]{:S(2)}) collective-permute-start(bf16[2,2,256,128]{3,2,1,0:T(8,128)(2,1)S(1)} %head_slices.3), channel_id=1, source_target_pairs={{0,6},{1,7},{2,4},{3,5},{4,2},{5,3},{6,0},{7,1},{8,14},{9,15},{10,... | collective-permute-start | bytes 786440 | tf_op jit(solution)/shard_map/ppermute | solution.py:469
  13.9 15.5 %collective-permute-start.1 = (bf16[2,2,256,128]{3,2,1,0:T(8,128)(2,1)S(1)}, bf16[2,2,256,128]{3,2,1,0:T(8,128)(2,1)S(1)}, u32[]{:S(2)}, u32[]{:S(2)}) collective-permute-start(bf16[2,2,256,128]{3,2,1,0:T(8,128)(2,1)S(1)} %get-tuple-element.24), channel_id=1, source_target_pairs={{0,7},{1,6},{2,5},{3,4},{4,3},{5,2},{6,1},{7,0},{8,15},{9,14},{10,... | collective-permute-start | bytes 786440 | tf_op jit(solution)/shard_map/ppermute | solution.py:469
  13.9 34.0 %copy-start = (bf16[2,4,1024]{2,1,0:T(4,128)(2,1)S(1)}, bf16[2,4,1024]{2,1,0:T(4,128)(2,1)}, u32[]{:S(2)}) copy-start(bf16[2,4,1024]{2,1,0:T(4,128)(2,1)} %new_keys_ref.1) | copy-start | bytes 49156
  13.9 34.0 %copy-start.1 = (bf16[2,4,1024]{2,1,0:T(4,128)(2,1)S(1)}, bf16[2,4,1024]{2,1,0:T(4,128)(2,1)}, u32[]{:S(2)}) copy-start(bf16[2,4,1024]{2,1,0:T(4,128)(2,1)} %new_values_ref.1) | copy-start | bytes 49156
  13.9 34.0 %copy-start.2 = (s32[2]{0:T(128)S(1)}, s32[2]{0:T(128)}, u32[]{:S(2)}) copy-start(s32[2]{0:T(128)} %len_ref.1) | copy-start | bytes 28
  13.9 20.8 %collective-permute-start.4 = (bf16[2,2,256,128]{3,2,1,0:T(8,128)(2,1)S(1)}, bf16[2,2,256,128]{3,2,1,0:T(8,128)(2,1)S(1)}, u32[]{:S(2)}, u32[]{:S(2)}) collective-permute-start(bf16[2,2,256,128]{3,2,1,0:T(8,128)(2,1)S(1)} %get-tuple-element.27), channel_id=1, source_target_pairs={{0,2},{1,3},{2,0},{3,1},{4,6},{5,7},{6,4},{7,5},{8,10},{9,11},{10,... | collective-permute-start | bytes 786440 | tf_op jit(solution)/shard_map/ppermute | solution.py:469
  17.6 17.2 %collective-permute-start.2 = (bf16[2,2,256,128]{3,2,1,0:T(8,128)(2,1)}, bf16[2,2,256,128]{3,2,1,0:T(8,128)(2,1)S(1)}, u32[]{:S(2)}, u32[]{:S(2)}) collective-permute-start(bf16[2,2,256,128]{3,2,1,0:T(8,128)(2,1)} %get-tuple-element.25), channel_id=1, source_target_pairs={{0,1},{1,0},{2,3},{3,2},{4,5},{5,4},{6,7},{7,6},{8,9},{9,8},{10,11... | collective-permute-start | bytes 786440 | tf_op jit(solution)/shard_map/ppermute | solution.py:469
  18.0 17.0 %collective-permute-start.3 = (bf16[2,2,256,128]{3,2,1,0:T(8,128)(2,1)S(1)}, bf16[2,2,256,128]{3,2,1,0:T(8,128)(2,1)S(1)}, u32[]{:S(2)}, u32[]{:S(2)}) collective-permute-start(bf16[2,2,256,128]{3,2,1,0:T(8,128)(2,1)S(1)} %get-tuple-element.26), channel_id=1, source_target_pairs={{0,4},{1,5},{2,6},{3,7},{4,0},{5,1},{6,2},{7,3},{8,12},{9,13},{10,... | collective-permute-start | bytes 786440 | tf_op jit(solution)/shard_map/ppermute | solution.py:469
  25.0 14.9 %collective-permute-start.5 = (bf16[2,2,256,128]{3,2,1,0:T(8,128)(2,1)S(1)}, bf16[2,2,256,128]{3,2,1,0:T(8,128)(2,1)S(1)}, u32[]{:S(2)}, u32[]{:S(2)}) collective-permute-start(bf16[2,2,256,128]{3,2,1,0:T(8,128)(2,1)S(1)} %get-tuple-element.32), channel_id=1, source_target_pairs={{0,3},{1,2},{2,1},{3,0},{4,7},{5,6},{6,5},{7,4},{8,11},{9,10},{10,... | collective-permute-start | bytes 786440 | tf_op jit(solution)/shard_map/ppermute | solution.py:469
  29.4 11.2 %collective-permute-start.6 = (bf16[2,2,256,128]{3,2,1,0:T(8,128)(2,1)S(1)}, bf16[2,2,256,128]{3,2,1,0:T(8,128)(2,1)S(1)}, u32[]{:S(2)}, u32[]{:S(2)}) collective-permute-start(bf16[2,2,256,128]{3,2,1,0:T(8,128)(2,1)S(1)} %get-tuple-element.36), channel_id=1, source_target_pairs={{0,5},{1,4},{2,7},{3,6},{4,1},{5,0},{6,3},{7,2},{8,13},{9,12},{10,... | collective-permute-start | bytes 786440 | tf_op jit(solution)/shard_map/ppermute | solution.py:469
  43.1 15.3 %all-to-all-start.1 = ((s16[16,72,128]{2,1,0:T(8,128)(2,1)}), s16[16,72,128]{2,1,0:T(8,128)(2,1)S(1)}, u32[]{:S(2)}, u32[]{:S(2)}) async-start(s16[16,72,128]{2,1,0:T(8,128)(2,1)} %last_stage.1), calls=%async_computation.1 | async-start | bytes 589824 | tf_op jit(solution)/shard_map/all_to_all | solution.py:492
where the time goes:
time: 60 us; the launch traced here: 59.6 us
  starting transfers between devices  20.1 us (34%)
  Pallas kernels  19.9 us (33%)
  waiting for transfers between devices  19.1 us (32%)
    ppermute x7, waiting for transfers between devices, exchange(): arrived[partner] = near(lax.ppermute(piece, 'seq', route))  13.1 us
    ppermute x7, starting transfers between devices, exchange(): arrived[partner] = near(lax.ppermute(piece, 'seq', route))  7.93 us
    all_to_all x1, starting transfers between devices, body(): lax.all_to_all(packed, 'seq', split_axis=0, concat_axis=0, tiled=True)  7.43 us
    pallas_call x1, Pallas kernels, suffix_part(): pl.pallas_call(suffix_kernel, out_shape=[jax.ShapeDtypeStruct((KEY_VALUE_...  6.16 us
    all_to_all x1, starting transfers between devices, body(): lax.all_to_all(sent, 'seq', split_axis=0, concat_axis=0, tiled=True)  4.79 us
    all_to_all x1, waiting for transfers between devices, body(): lax.all_to_all(sent, 'seq', split_axis=0, concat_axis=0, tiled=True)  4.34 us
    pallas_call x1, Pallas kernels, first_stage(): pl.pallas_call(functools.partial(first_kernel, rows, min(512, total // pr...  3.66 us
    pallas_call x2, Pallas kernels, head_slices(): pl.pallas_call(functools.partial(slice_kernel, partners), out_shape=[piec...  3.18 us
  transfers between devices with their start and end apart: 9, of which 7 were waited for; matrix products, arithmetic and copies ran while one was open for 1% of the time, Pallas kernels for 23%

commit v1 on v0

--- a/solution.py
+++ b/solution.py
@@ -17,7 +17,8 @@
 LANES = 128
 FIRST = (6,)
 EARLY = (7, 2)
-LATE = (4, 5, 3, 1)
+SOON = (4,)
+LATE = (5, 3, 1)
 LIMIT = pltpu.CompilerParams(vmem_limit_bytes=24 * 1024 * 1024)
 LEVELS = 32767.0
 CODE_STEPS = 256.0
@@ -476,16 +477,19 @@
     for partner, piece in zip(EARLY, slices):
         exchange(piece, partner)
     head_queries = lax.all_to_all(packed, "seq", split_axis=0, concat_axis=0, tiled=True)
+    soon = head_slices(document_keys, document_values, SOON)
+    for partner, piece in zip(SOON, soon):
+        exchange(piece, partner)
     slices = head_slices(document_keys, document_values, LATE + (0,))
     arrived[0] = near(slices[-1])
     for partner, piece in zip(LATE, slices):
         exchange(piece, partner)
     head_ids = head_queries[:, owned * rows, :owned].reshape(-1).astype(jnp.int32)
     places = find_places(head_ids, document_keys.shape[0], rows)
-    ready = [arrived[k] for k in (0, 6, 7, 1, 4, 2)]
+    ready = [arrived[k] for k in (0, 6, 7, 1, 2)]
     state = first_stage(places, near(head_queries), ready, rows)
-    state = next_stage(state, [arrived[3]])
-    sent = last_stage(places, state, [arrived[5]], rows, devices)
+    state = next_stage(state, [arrived[k] for k in (4,)])
+    sent = last_stage(places, state, [arrived[k] for k in (5, 3)], rows, devices)
     local, local_aux = suffix_part(
         suffix_len, packed, far(sample_keys), far(sample_values), step_keys, step_values
     )

time: 60 us -> 59.8 us (level)
  starting transfers between devices: 20.1 us -> 19.1 us
  Pallas kernels: 19.9 us -> 20.5 us
    ppermute x7, waiting for transfers between devices: 13.1 us -> 14.6 us  [exchange(): arrived[partner] = near(lax.ppermute(piece, 'seq', route))]
    all_to_all x1, waiting for transfers between devices: 1.64 us -> 0.37 us  [body(): lax.all_to_all(packed, 'seq', split_axis=0, concat_axis=0, tiled=True)]
    pallas_call x2 -> x3, Pallas kernels: 3.18 us -> 4.07 us  [head_slices(): pl.pallas_call(functools.partial(slice_kernel, partners), out_shape=[piec...]
    ppermute x7, starting transfers between devices: 7.93 us -> 7.24 us  [exchange(): arrived[partner] = near(lax.ppermute(piece, 'seq', route))]
    pallas_call x1, Pallas kernels: 3.66 us -> 3.01 us  [first_stage(): pl.pallas_call(functools.partial(first_kernel, rows, min(512, total // pr...]
  transfers between devices with their start and end apart: 9 -> 9, of which waited for: 7 -> 6; matrix products, arithmetic and copies ran while one was open for 1% -> 1% of each run, Pallas kernels for 23% -> 23%
where the time goes in v1:
time: 59.8 us; the launch traced here: 59.4 us
  Pallas kernels  20.5 us (34%)
  waiting for transfers between devices  19.3 us (32%)
  starting transfers between devices  19.1 us (32%)
    ppermute x7, waiting for transfers between devices, exchange(): arrived[partner] = near(lax.ppermute(piece, 'seq', route))  14.6 us
    all_to_all x1, starting transfers between devices, body(): lax.all_to_all(packed, 'seq', split_axis=0, concat_axis=0, tiled=True)  7.43 us
    ppermute x7, starting transfers between devices, exchange(): arrived[partner] = near(lax.ppermute(piece, 'seq', route))  7.24 us
    pallas_call x1, Pallas kernels, suffix_part(): pl.pallas_call(suffix_kernel, out_shape=[jax.ShapeDtypeStruct((KEY_VALUE_...  6.16 us
    all_to_all x1, starting transfers between devices, body(): lax.all_to_all(sent, 'seq', split_axis=0, concat_axis=0, tiled=True)  4.45 us
    all_to_all x1, waiting for transfers between devices, body(): lax.all_to_all(sent, 'seq', split_axis=0, concat_axis=0, tiled=True)  4.34 us
    pallas_call x3, Pallas kernels, head_slices(): pl.pallas_call(functools.partial(slice_kernel, partners), out_shape=[piec...  4.07 us
    pallas_call x1, Pallas kernels, first_stage(): pl.pallas_call(functools.partial(first_kernel, rows, min(512, total // pr...  3.01 us
  transfers between devices with their start and end apart: 9, of which 6 were waited for; matrix products, arithmetic and copies ran while one was open for 1% of the time, Pallas kernels for 23%

profile of v1, /device:TPU:0, one launch (start us, length us, event | category | flops | bytes accessed | tf_op | source)
XLA Modules:
  0.0 59.4 jit_solution(11302616655713634963)
XLA Ops:
  0.0 2.6 %slices_and_queries.1 = (bf16[2,2,256,128]{3,2,1,0:T(8,128)(2,1)S(1)}, bf16[2,2,256,128]{3,2,1,0:T(8,128)(2,1)S(1)}, bf16[16,72,128]{2,1,0:T(8,128)(2,1)}) custom-call(bf16[2,256,1024]{2,1,0:T(8,128)(2,1)} %keys_ref.7, bf16[2,256,1024]{2,1,0:T(8,128)(2,1)} %values_ref.7, s32[2]{0:T(128)} %ids_ref.1, bf16[2,4,8192]{2,1,0:T(4,128)(2,1)} %queries_ref.1), custom_call_target="tpu_custom_call" | custom-call | tf_op jit(solution)/shard_map/slices_and_queries/pallas_call | solution.py:115
  2.6 7.4 %all-to-all-start = ((bf16[16,72,128]{2,1,0:T(8,128)(2,1)}), bf16[16,72,128]{2,1,0:T(8,128)(2,1)S(1)}, u32[]{:S(2)}, u32[]{:S(2)}) async-start(bf16[16,72,128]{2,1,0:T(8,128)(2,1)} %get-tuple-element.21.query_ref), calls=%async_computation | async-start | bytes 589824 | tf_op jit(solution)/shard_map/all_to_all | solution.py:479
  10.0 2.1 %head_slices.3 = (bf16[2,2,256,128]{3,2,1,0:T(8,128)(2,1)S(1)}, bf16[2,2,256,128]{3,2,1,0:T(8,128)(2,1)S(1)}, bf16[2,2,256,128]{3,2,1,0:T(8,128)(2,1)}, bf16[2,2,256,128]{3,2,1,0:T(8,128)(2,1)S(1)}) custom-call(bf16[2,256,1024]{2,1,0:T(8,128)(2,1)} %keys_ref.7, bf16[2,256,1024]{2,1,0:T(8,128)(2,1)} %values_ref.7), custom_call_target="tpu_custom_call" | custom-call | tf_op jit(solution)/shard_map/head_slices/pallas_call | solution.py:67
  12.1 0.5 collective-permute-start.2
  12.6 2.5 %collective-permute-start.1 = (bf16[2,2,256,128]{3,2,1,0:T(8,128)(2,1)S(1)}, bf16[2,2,256,128]{3,2,1,0:T(8,128)(2,1)S(1)}, u32[]{:S(2)}, u32[]{:S(2)}) collective-permute-start(bf16[2,2,256,128]{3,2,1,0:T(8,128)(2,1)S(1)} %get-tuple-element.23), channel_id=1, source_target_pairs={{0,7},{1,6},{2,5},{3,4},{4,3},{5,2},{6,1},{7,0},{8,15},{9,14},{10,... | collective-permute-start | bytes 786440 | tf_op jit(solution)/shard_map/ppermute | solution.py:470
  15.1 0.6 collective-permute-start.3
  15.7 1.0 %head_slices.4 = bf16[2,2,256,128]{3,2,1,0:T(8,128)(2,1)S(1)} custom-call(bf16[2,256,1024]{2,1,0:T(8,128)(2,1)} %keys_ref.7, bf16[2,256,1024]{2,1,0:T(8,128)(2,1)} %values_ref.7), custom_call_target="tpu_custom_call" | custom-call | tf_op jit(solution)/shard_map/head_slices/pallas_call | solution.py:67
  16.7 0.0 copy-start
  16.7 0.0 copy-start.1
  16.7 0.0 copy-start.2
  16.7 1.5 %collective-permute-start = (bf16[2,2,256,128]{3,2,1,0:T(8,128)(2,1)S(1)}, bf16[2,2,256,128]{3,2,1,0:T(8,128)(2,1)S(1)}, u32[]{:S(2)}, u32[]{:S(2)}) collective-permute-start(bf16[2,2,256,128]{3,2,1,0:T(8,128)(2,1)S(1)} %head_slices.4), channel_id=1, source_target_pairs={{0,6},{1,7},{2,4},{3,5},{4,2},{5,3},{6,0},{7,1},{8,14},{9,15},{10,... | collective-permute-start | bytes 786440 | tf_op jit(solution)/shard_map/ppermute | solution.py:470
  18.3 1.0 %head_slices.5 = bf16[2,2,256,128]{3,2,1,0:T(8,128)(2,1)S(1)} custom-call(bf16[2,256,1024]{2,1,0:T(8,128)(2,1)} %keys_ref.7, bf16[2,256,1024]{2,1,0:T(8,128)(2,1)} %values_ref.7), custom_call_target="tpu_custom_call" | custom-call | tf_op jit(solution)/shard_map/head_slices/pallas_call | solution.py:67
  19.3 1.5 %collective-permute-start.4 = (bf16[2,2,256,128]{3,2,1,0:T(8,128)(2,1)S(1)}, bf16[2,2,256,128]{3,2,1,0:T(8,128)(2,1)S(1)}, u32[]{:S(2)}, u32[]{:S(2)}) collective-permute-start(bf16[2,2,256,128]{3,2,1,0:T(8,128)(2,1)S(1)} %head_slices.5), channel_id=1, source_target_pairs={{0,4},{1,5},{2,6},{3,7},{4,0},{5,1},{6,2},{7,3},{8,12},{9,13},{10,... | collective-permute-start | bytes 786440 | tf_op jit(solution)/shard_map/ppermute | solution.py:470
  20.8 0.4 all-to-all-done.queries_ref
  21.2 0.1 reshape.12
  21.3 0.0 collective-permute-done.2.refs_3_
  21.3 0.2 collective-permute-start.5
  21.4 3.0 %collective-permute-done.1.refs_2_ = bf16[2,2,256,128]{3,2,1,0:T(8,128)(2,1)S(1)} collective-permute-done((bf16[2,2,256,128]{3,2,1,0:T(8,128)(2,1)S(1)}, bf16[2,2,256,128]{3,2,1,0:T(8,128)(2,1)S(1)}, u32[]{:S(2)}, u32[]{:S(2)}) %collective-permute-start.1) | collective-permute-done | bytes 262176 | tf_op jit(solution)/shard_map/ppermute | solution.py:470
  24.4 0.5 collective-permute-start.6
  24.9 0.2 convert_reduce_fusion
  25.1 10.2 %collective-permute-done.3.refs_4_ = bf16[2,2,256,128]{3,2,1,0:T(8,128)(2,1)S(1)} collective-permute-done((bf16[2,2,256,128]{3,2,1,0:T(8,128)(2,1)S(1)}, bf16[2,2,256,128]{3,2,1,0:T(8,128)(2,1)S(1)}, u32[]{:S(2)}, u32[]{:S(2)}) %collective-permute-start.3) | collective-permute-done | bytes 262176 | tf_op jit(solution)/shard_map/ppermute | solution.py:470
  35.3 0.0 collective-permute-done.refs_1_
  35.3 3.0 %first_stage.1 = (bf16[1024,128]{1,0:T(8,128)(2,1)S(1)}, f32[1024,128]{1,0:T(8,128)S(1)}, f32[1024,128]{1,0:T(8,128)S(1)}, f32[1024,128]{1,0:T(8,128)S(1)}) custom-call(s32[32]{0:T(128)S(1)} %add_multiply_fusion.place_ref, bf16[16,72,128]{2,1,0:T(8,128)(2,1)S(1)} %all-to-all-done.queries_ref, bf16[2,2,256,128]{3,2,1,0:T(8,128)(2,1)S(1)} %get-tuple-element.22.refs_0_, ...), custom_call_target="tpu_custom_call" | custom-call | tf_op jit(solution)/shard_map/first_stage/pallas_call | solution.py:357
  38.3 0.0 collective-permute-done.4.refs_0_
  38.3 0.7 %next_stage.1 = (f32[1024,128]{1,0:T(8,128)S(1)}, f32[1024,128]{1,0:T(8,128)S(1)}, f32[1024,128]{1,0:T(8,128)S(1)}) custom-call(bf16[1024,128]{1,0:T(8,128)(2,1)S(1)} %get-tuple-element.26.sorted_ref, f32[1024,128]{1,0:T(8,128)S(1)} %get-tuple-element.27.acc_in, f32[1024,128]{1,0:T(8,128)S(1)} %get-tuple-element.28.peak_in, ...), custom_call_target="tpu_custom_call" | custom-call | tf_op jit(solution)/shard_map/next_stage/pallas_call | solution.py:376
  39.0 1.4 %collective-permute-done.5.refs_0_ = bf16[2,2,256,128]{3,2,1,0:T(8,128)(2,1)S(1)} collective-permute-done((bf16[2,2,256,128]{3,2,1,0:T(8,128)(2,1)S(1)}, bf16[2,2,256,128]{3,2,1,0:T(8,128)(2,1)S(1)}, u32[]{:S(2)}, u32[]{:S(2)}) %collective-permute-start.5) | collective-permute-done | bytes 262176 | tf_op jit(solution)/shard_map/ppermute | solution.py:470
  40.4 0.1 collective-permute-done.6.refs_1_
  40.4 2.8 %last_stage.1 = s16[16,72,128]{2,1,0:T(8,128)(2,1)} custom-call(s32[32]{0:T(128)S(1)} %add_multiply_fusion.place_ref, bf16[1024,128]{1,0:T(8,128)(2,1)S(1)} %get-tuple-element.26.sorted_ref, f32[1024,128]{1,0:T(8,128)S(1)} %get-tuple-element.30.acc_ref, f32[1024,128]{1,0:T(8,128)S(1)} %get-tuple-element.31.peak_ref, ...), custom_call_target="tpu_custom_call" | custom-call | tf_op jit(solution)/shard_map/last_stage/pallas_call | solution.py:390
  43.2 4.4 %all-to-all-start.1 = ((s16[16,72,128]{2,1,0:T(8,128)(2,1)}), s16[16,72,128]{2,1,0:T(8,128)(2,1)S(1)}, u32[]{:S(2)}, u32[]{:S(2)}) async-start(s16[16,72,128]{2,1,0:T(8,128)(2,1)} %last_stage.1), calls=%async_computation.1 | async-start | bytes 589824 | tf_op jit(solution)/shard_map/all_to_all | solution.py:496
  47.7 6.2 %suffix_part.1 = (f32[8,64,128]{2,1,0:T(8,128)S(1)}, f32[8,1,128]{2,1,0:T(1,128)S(1)}) custom-call(s32[2]{0:T(128)S(1)} %copy-done.2, bf16[16,72,128]{2,1,0:T(8,128)(2,1)} %get-tuple-element.21.query_ref, bf16[2,1024,1024]{2,1,0:T(8,128)(2,1)} %keys_hbm.1, bf16[2,1024,1024]{2,1,0:T(8,128)(2,1)} %values_hbm.1, bf16[2,4,1024]{2,1,0:T(4,128)(2,1)S(1)} %copy-done, ...), custom_call_target="tpu_custom_call" | custom-call | tf_op jit(solution)/shard_map/suffix_part/pallas_call | solution.py:218
  53.9 4.3 %all-to-all-done.1.got_ref = s16[16,72,128]{2,1,0:T(8,128)(2,1)S(1)} async-done(((s16[16,72,128]{2,1,0:T(8,128)(2,1)}), s16[16,72,128]{2,1,0:T(8,128)(2,1)S(1)}, u32[]{:S(2)}, u32[]{:S(2)}) %all-to-all-start.1) | async-done | bytes 294944 | tf_op jit(solution)/shard_map/all_to_all | solution.py:496
  58.2 1.1 %merge.1 = bf16[2,4,8192]{2,1,0:T(4,128)(2,1)} custom-call(s16[16,72,128]{2,1,0:T(8,128)(2,1)S(1)} %all-to-all-done.1.got_ref, f32[8,64,128]{2,1,0:T(8,128)S(1)} %get-tuple-element.35.local_ref, f32[8,1,128]{2,1,0:T(1,128)S(1)} %get-tuple-element.36.local_aux_ref), custom_call_target="tpu_custom_call" | custom-call | tf_op jit(solution)/shard_map/merge/pallas_call | solution.py:441
  (5 shorter events, 0.0 us)
Async XLA Ops:
  2.6 18.5 %all-to-all-start = ((bf16[16,72,128]{2,1,0:T(8,128)(2,1)}), bf16[16,72,128]{2,1,0:T(8,128)(2,1)S(1)}, u32[]{:S(2)}, u32[]{:S(2)}) async-start(bf16[16,72,128]{2,1,0:T(8,128)(2,1)} %get-tuple-element.21.query_ref), calls=%async_computation | async-start | bytes 589824 | tf_op jit(solution)/shard_map/all_to_all | solution.py:479
  12.1 9.1 %collective-permute-start.2 = (bf16[2,2,256,128]{3,2,1,0:T(8,128)(2,1)}, bf16[2,2,256,128]{3,2,1,0:T(8,128)(2,1)S(1)}, u32[]{:S(2)}, u32[]{:S(2)}) collective-permute-start(bf16[2,2,256,128]{3,2,1,0:T(8,128)(2,1)} %get-tuple-element.24), channel_id=1, source_target_pairs={{0,1},{1,0},{2,3},{3,2},{4,5},{5,4},{6,7},{7,6},{8,9},{9,8},{10,11... | collective-permute-start | bytes 786440 | tf_op jit(solution)/shard_map/ppermute | solution.py:470
  12.6 11.8 %collective-permute-start.1 = (bf16[2,2,256,128]{3,2,1,0:T(8,128)(2,1)S(1)}, bf16[2,2,256,128]{3,2,1,0:T(8,128)(2,1)S(1)}, u32[]{:S(2)}, u32[]{:S(2)}) collective-permute-start(bf16[2,2,256,128]{3,2,1,0:T(8,128)(2,1)S(1)} %get-tuple-element.23), channel_id=1, source_target_pairs={{0,7},{1,6},{2,5},{3,4},{4,3},{5,2},{6,1},{7,0},{8,15},{9,14},{10,... | collective-permute-start | bytes 786440 | tf_op jit(solution)/shard_map/ppermute | solution.py:470
  15.1 20.1 %collective-permute-start.3 = (bf16[2,2,256,128]{3,2,1,0:T(8,128)(2,1)S(1)}, bf16[2,2,256,128]{3,2,1,0:T(8,128)(2,1)S(1)}, u32[]{:S(2)}, u32[]{:S(2)}) collective-permute-start(bf16[2,2,256,128]{3,2,1,0:T(8,128)(2,1)S(1)} %get-tuple-element.25), channel_id=1, source_target_pairs={{0,2},{1,3},{2,0},{3,1},{4,6},{5,7},{6,4},{7,5},{8,10},{9,11},{10,... | collective-permute-start | bytes 786440 | tf_op jit(solution)/shard_map/ppermute | solution.py:470
  16.7 31.0 %copy-start = (bf16[2,4,1024]{2,1,0:T(4,128)(2,1)S(1)}, bf16[2,4,1024]{2,1,0:T(4,128)(2,1)}, u32[]{:S(2)}) copy-start(bf16[2,4,1024]{2,1,0:T(4,128)(2,1)} %new_keys_ref.1) | copy-start | bytes 49156
  16.7 31.0 %copy-start.1 = (bf16[2,4,1024]{2,1,0:T(4,128)(2,1)S(1)}, bf16[2,4,1024]{2,1,0:T(4,128)(2,1)}, u32[]{:S(2)}) copy-start(bf16[2,4,1024]{2,1,0:T(4,128)(2,1)} %new_values_ref.1) | copy-start | bytes 49156
  16.7 31.0 %copy-start.2 = (s32[2]{0:T(128)S(1)}, s32[2]{0:T(128)}, u32[]{:S(2)}) copy-start(s32[2]{0:T(128)} %len_ref.1) | copy-start | bytes 28
  16.7 18.5 %collective-permute-start = (bf16[2,2,256,128]{3,2,1,0:T(8,128)(2,1)S(1)}, bf16[2,2,256,128]{3,2,1,0:T(8,128)(2,1)S(1)}, u32[]{:S(2)}, u32[]{:S(2)}) collective-permute-start(bf16[2,2,256,128]{3,2,1,0:T(8,128)(2,1)S(1)} %head_slices.4), channel_id=1, source_target_pairs={{0,6},{1,7},{2,4},{3,5},{4,2},{5,3},{6,0},{7,1},{8,14},{9,15},{10,... | collective-permute-start | bytes 786440 | tf_op jit(solution)/shard_map/ppermute | solution.py:470
  19.3 19.0 %collective-permute-start.4 = (bf16[2,2,256,128]{3,2,1,0:T(8,128)(2,1)S(1)}, bf16[2,2,256,128]{3,2,1,0:T(8,128)(2,1)S(1)}, u32[]{:S(2)}, u32[]{:S(2)}) collective-permute-start(bf16[2,2,256,128]{3,2,1,0:T(8,128)(2,1)S(1)} %head_slices.5), channel_id=1, source_target_pairs={{0,4},{1,5},{2,6},{3,7},{4,0},{5,1},{6,2},{7,3},{8,12},{9,13},{10,... | collective-permute-start | bytes 786440 | tf_op jit(solution)/shard_map/ppermute | solution.py:470
  21.3 19.1 %collective-permute-start.5 = (bf16[2,2,256,128]{3,2,1,0:T(8,128)(2,1)S(1)}, bf16[2,2,256,128]{3,2,1,0:T(8,128)(2,1)S(1)}, u32[]{:S(2)}, u32[]{:S(2)}) collective-permute-start(bf16[2,2,256,128]{3,2,1,0:T(8,128)(2,1)S(1)} %get-tuple-element.33), channel_id=1, source_target_pairs={{0,5},{1,4},{2,7},{3,6},{4,1},{5,0},{6,3},{7,2},{8,13},{9,12},{10,... | collective-permute-start | bytes 786440 | tf_op jit(solution)/shard_map/ppermute | solution.py:470
  24.4 16.0 %collective-permute-start.6 = (bf16[2,2,256,128]{3,2,1,0:T(8,128)(2,1)S(1)}, bf16[2,2,256,128]{3,2,1,0:T(8,128)(2,1)S(1)}, u32[]{:S(2)}, u32[]{:S(2)}) collective-permute-start(bf16[2,2,256,128]{3,2,1,0:T(8,128)(2,1)S(1)} %get-tuple-element.34), channel_id=1, source_target_pairs={{0,3},{1,2},{2,1},{3,0},{4,7},{5,6},{6,5},{7,4},{8,11},{9,10},{10,... | collective-permute-start | bytes 786440 | tf_op jit(solution)/shard_map/ppermute | solution.py:470
  43.2 15.0 %all-to-all-start.1 = ((s16[16,72,128]{2,1,0:T(8,128)(2,1)}), s16[16,72,128]{2,1,0:T(8,128)(2,1)S(1)}, u32[]{:S(2)}, u32[]{:S(2)}) async-start(s16[16,72,128]{2,1,0:T(8,128)(2,1)} %last_stage.1), calls=%async_computation.1 | async-start | bytes 589824 | tf_op jit(solution)/shard_map/all_to_all | solution.py:496

commit v2 on v1

--- a/solution.py
+++ b/solution.py
@@ -26,6 +26,7 @@
 TINY = 2.0**-100
 AUX_ROWS = 8
 LOAD_PARTS = 4
+PACKED = pltpu.CompilerParams(vmem_limit_bytes=24 * 1024 * 1024)
 WEIGHT_SCALE = SCALING * math.log2(math.e)
 
 
@@ -348,7 +349,7 @@
         out_ref[device, owned * rows :, :] = to_words(words)
         return carry
 
-    lax.fori_loop(0, devices, emit, 0, unroll=4)
+    lax.fori_loop(0, devices, emit, 0, unroll=16)
 
 
 def first_stage(places, queries, pieces, rows):
@@ -364,7 +365,7 @@
         ],
         in_specs=[whole(pltpu.SMEM)] + [whole()] * (1 + len(pieces)),
         out_specs=[whole()] * 4,
-        compiler_params=LIMIT,
+        compiler_params=PACKED,
         name="first_stage",
     )(places, queries, *pieces)
     return [near(result) for result in results]
@@ -378,7 +379,7 @@
         out_shape=[jax.ShapeDtypeStruct((total, HEAD_SIZE), jnp.float32)] * 3,
         in_specs=[whole()] * (4 + len(pieces)),
         out_specs=[whole()] * 3,
-        compiler_params=LIMIT,
+        compiler_params=PACKED,
         name="next_stage",
     )(*state, *pieces)
     return [state[0]] + [near(result) for result in results]
@@ -396,7 +397,7 @@
             pltpu.VMEM((total, HEAD_SIZE), jnp.int16),
             pltpu.VMEM((total, HEAD_SIZE), jnp.float32),
         ],
-        compiler_params=LIMIT,
+        compiler_params=PACKED,
         name="last_stage",
     )(places, *state, *pieces)
 
@@ -443,7 +444,7 @@
         out_shape=jax.ShapeDtypeStruct(shape, jnp.bfloat16),
         in_specs=[whole()] * 3,
         out_specs=whole(),
-        compiler_params=LIMIT,
+        compiler_params=PACKED,
         name="merge",
     )(got, local, local_aux)
 

time: 59.8 us -> 59.7 us (level)
  transfers between devices with their start and end apart: 9 -> 9, of which waited for: 6 -> 6; matrix products, arithmetic and copies ran while one was open for 1% -> 1% of each run, Pallas kernels for 23% -> 24%
where the time goes in v2:
time: 59.7 us; the launch traced here: 59.3 us
  Pallas kernels  20.4 us (34%)
  waiting for transfers between devices  19.3 us (32%)
  starting transfers between devices  19.1 us (32%)
    ppermute x7, waiting for transfers between devices, exchange(): arrived[partner] = near(lax.ppermute(piece, 'seq', route))  14.6 us
    all_to_all x1, starting transfers between devices, body(): lax.all_to_all(packed, 'seq', split_axis=0, concat_axis=0, tiled=True)  7.43 us
    ppermute x7, starting transfers between devices, exchange(): arrived[partner] = near(lax.ppermute(piece, 'seq', route))  7.24 us
    pallas_call x1, Pallas kernels, suffix_part(): pl.pallas_call(suffix_kernel, out_shape=[jax.ShapeDtypeStruct((KEY_VALUE_...  6.16 us
    all_to_all x1, starting transfers between devices, body(): lax.all_to_all(sent, 'seq', split_axis=0, concat_axis=0, tiled=True)  4.45 us
    all_to_all x1, waiting for transfers between devices, body(): lax.all_to_all(sent, 'seq', split_axis=0, concat_axis=0, tiled=True)  4.34 us
    pallas_call x3, Pallas kernels, head_slices(): pl.pallas_call(functools.partial(slice_kernel, partners), out_shape=[piec...  4.07 us
    pallas_call x1, Pallas kernels, first_stage(): pl.pallas_call(functools.partial(first_kernel, rows, min(512, total // pr...  3.01 us
  transfers between devices with their start and end apart: 9, of which 6 were waited for; matrix products, arithmetic and copies ran while one was open for 1% of the time, Pallas kernels for 24%

profile of v2, /device:TPU:0, one launch (start us, length us, event | category | flops | bytes accessed | tf_op | source)
XLA Modules:
  0.0 59.3 jit_solution(12693962889604136285)
XLA Ops:
  0.0 2.6 %slices_and_queries.1 = (bf16[2,2,256,128]{3,2,1,0:T(8,128)(2,1)S(1)}, bf16[2,2,256,128]{3,2,1,0:T(8,128)(2,1)S(1)}, bf16[16,72,128]{2,1,0:T(8,128)(2,1)}) custom-call(bf16[2,256,1024]{2,1,0:T(8,128)(2,1)} %keys_ref.7, bf16[2,256,1024]{2,1,0:T(8,128)(2,1)} %values_ref.7, s32[2]{0:T(128)} %ids_ref.1, bf16[2,4,8192]{2,1,0:T(4,128)(2,1)} %queries_ref.1), custom_call_target="tpu_custom_call" | custom-call | tf_op jit(solution)/shard_map/slices_and_queries/pallas_call | solution.py:116
  2.6 7.4 %all-to-all-start = ((bf16[16,72,128]{2,1,0:T(8,128)(2,1)}), bf16[16,72,128]{2,1,0:T(8,128)(2,1)S(1)}, u32[]{:S(2)}, u32[]{:S(2)}) async-start(bf16[16,72,128]{2,1,0:T(8,128)(2,1)} %get-tuple-element.21.query_ref), calls=%async_computation | async-start | bytes 589824 | tf_op jit(solution)/shard_map/all_to_all | solution.py:480
  10.0 2.1 %head_slices.3 = (bf16[2,2,256,128]{3,2,1,0:T(8,128)(2,1)S(1)}, bf16[2,2,256,128]{3,2,1,0:T(8,128)(2,1)S(1)}, bf16[2,2,256,128]{3,2,1,0:T(8,128)(2,1)}, bf16[2,2,256,128]{3,2,1,0:T(8,128)(2,1)S(1)}) custom-call(bf16[2,256,1024]{2,1,0:T(8,128)(2,1)} %keys_ref.7, bf16[2,256,1024]{2,1,0:T(8,128)(2,1)} %values_ref.7), custom_call_target="tpu_custom_call" | custom-call | tf_op jit(solution)/shard_map/head_slices/pallas_call | solution.py:68
  12.1 0.5 collective-permute-start.2
  12.6 2.5 %collective-permute-start.1 = (bf16[2,2,256,128]{3,2,1,0:T(8,128)(2,1)S(1)}, bf16[2,2,256,128]{3,2,1,0:T(8,128)(2,1)S(1)}, u32[]{:S(2)}, u32[]{:S(2)}) collective-permute-start(bf16[2,2,256,128]{3,2,1,0:T(8,128)(2,1)S(1)} %get-tuple-element.23), channel_id=1, source_target_pairs={{0,7},{1,6},{2,5},{3,4},{4,3},{5,2},{6,1},{7,0},{8,15},{9,14},{10,... | collective-permute-start | bytes 786440 | tf_op jit(solution)/shard_map/ppermute | solution.py:471
  15.1 0.6 collective-permute-start.3
  15.7 1.0 %head_slices.4 = bf16[2,2,256,128]{3,2,1,0:T(8,128)(2,1)S(1)} custom-call(bf16[2,256,1024]{2,1,0:T(8,128)(2,1)} %keys_ref.7, bf16[2,256,1024]{2,1,0:T(8,128)(2,1)} %values_ref.7), custom_call_target="tpu_custom_call" | custom-call | tf_op jit(solution)/shard_map/head_slices/pallas_call | solution.py:68
  16.7 0.0 copy-start
  16.7 0.0 copy-start.1
  16.7 0.0 copy-start.2
  16.7 1.5 %collective-permute-start = (bf16[2,2,256,128]{3,2,1,0:T(8,128)(2,1)S(1)}, bf16[2,2,256,128]{3,2,1,0:T(8,128)(2,1)S(1)}, u32[]{:S(2)}, u32[]{:S(2)}) collective-permute-start(bf16[2,2,256,128]{3,2,1,0:T(8,128)(2,1)S(1)} %head_slices.4), channel_id=1, source_target_pairs={{0,6},{1,7},{2,4},{3,5},{4,2},{5,3},{6,0},{7,1},{8,14},{9,15},{10,... | collective-permute-start | bytes 786440 | tf_op jit(solution)/shard_map/ppermute | solution.py:471
  18.3 1.0 %head_slices.5 = bf16[2,2,256,128]{3,2,1,0:T(8,128)(2,1)S(1)} custom-call(bf16[2,256,1024]{2,1,0:T(8,128)(2,1)} %keys_ref.7, bf16[2,256,1024]{2,1,0:T(8,128)(2,1)} %values_ref.7), custom_call_target="tpu_custom_call" | custom-call | tf_op jit(solution)/shard_map/head_slices/pallas_call | solution.py:68
  19.3 1.5 %collective-permute-start.4 = (bf16[2,2,256,128]{3,2,1,0:T(8,128)(2,1)S(1)}, bf16[2,2,256,128]{3,2,1,0:T(8,128)(2,1)S(1)}, u32[]{:S(2)}, u32[]{:S(2)}) collective-permute-start(bf16[2,2,256,128]{3,2,1,0:T(8,128)(2,1)S(1)} %head_slices.5), channel_id=1, source_target_pairs={{0,4},{1,5},{2,6},{3,7},{4,0},{5,1},{6,2},{7,3},{8,12},{9,13},{10,... | collective-permute-start | bytes 786440 | tf_op jit(solution)/shard_map/ppermute | solution.py:471
  20.8 0.4 all-to-all-done.queries_ref
  21.2 0.1 reshape.12
  21.3 0.0 collective-permute-done.2.refs_3_
  21.3 0.2 collective-permute-start.5
  21.4 3.0 %collective-permute-done.1.refs_2_ = bf16[2,2,256,128]{3,2,1,0:T(8,128)(2,1)S(1)} collective-permute-done((bf16[2,2,256,128]{3,2,1,0:T(8,128)(2,1)S(1)}, bf16[2,2,256,128]{3,2,1,0:T(8,128)(2,1)S(1)}, u32[]{:S(2)}, u32[]{:S(2)}) %collective-permute-start.1) | collective-permute-done | bytes 262176 | tf_op jit(solution)/shard_map/ppermute | solution.py:471
  24.4 0.5 collective-permute-start.6
  24.9 0.2 convert_reduce_fusion
  25.1 10.2 %collective-permute-done.3.refs_4_ = bf16[2,2,256,128]{3,2,1,0:T(8,128)(2,1)S(1)} collective-permute-done((bf16[2,2,256,128]{3,2,1,0:T(8,128)(2,1)S(1)}, bf16[2,2,256,128]{3,2,1,0:T(8,128)(2,1)S(1)}, u32[]{:S(2)}, u32[]{:S(2)}) %collective-permute-start.3) | collective-permute-done | bytes 262176 | tf_op jit(solution)/shard_map/ppermute | solution.py:471
  35.3 0.0 collective-permute-done.refs_1_
  35.3 3.0 %first_stage.1 = (bf16[1024,128]{1,0:T(8,128)(2,1)S(1)}, f32[1024,128]{1,0:T(8,128)S(1)}, f32[1024,128]{1,0:T(8,128)S(1)}, f32[1024,128]{1,0:T(8,128)S(1)}) custom-call(s32[32]{0:T(128)S(1)} %add_multiply_fusion.place_ref, bf16[16,72,128]{2,1,0:T(8,128)(2,1)S(1)} %all-to-all-done.queries_ref, bf16[2,2,256,128]{3,2,1,0:T(8,128)(2,1)S(1)} %get-tuple-element.22.refs_0_, ...), custom_call_target="tpu_custom_call" | custom-call | tf_op jit(solution)/shard_map/first_stage/pallas_call | solution.py:358
  38.3 0.0 collective-permute-done.4.refs_0_
  38.3 0.7 %next_stage.1 = (f32[1024,128]{1,0:T(8,128)S(1)}, f32[1024,128]{1,0:T(8,128)S(1)}, f32[1024,128]{1,0:T(8,128)S(1)}) custom-call(bf16[1024,128]{1,0:T(8,128)(2,1)S(1)} %get-tuple-element.26.sorted_ref, f32[1024,128]{1,0:T(8,128)S(1)} %get-tuple-element.27.acc_in, f32[1024,128]{1,0:T(8,128)S(1)} %get-tuple-element.28.peak_in, ...), custom_call_target="tpu_custom_call" | custom-call | tf_op jit(solution)/shard_map/next_stage/pallas_call | solution.py:377
  39.0 1.4 %collective-permute-done.5.refs_0_ = bf16[2,2,256,128]{3,2,1,0:T(8,128)(2,1)S(1)} collective-permute-done((bf16[2,2,256,128]{3,2,1,0:T(8,128)(2,1)S(1)}, bf16[2,2,256,128]{3,2,1,0:T(8,128)(2,1)S(1)}, u32[]{:S(2)}, u32[]{:S(2)}) %collective-permute-start.5) | collective-permute-done | bytes 262176 | tf_op jit(solution)/shard_map/ppermute | solution.py:471
  40.4 0.1 collective-permute-done.6.refs_1_
  40.4 2.8 %last_stage.1 = s16[16,72,128]{2,1,0:T(8,128)(2,1)} custom-call(s32[32]{0:T(128)S(1)} %add_multiply_fusion.place_ref, bf16[1024,128]{1,0:T(8,128)(2,1)S(1)} %get-tuple-element.26.sorted_ref, f32[1024,128]{1,0:T(8,128)S(1)} %get-tuple-element.30.acc_ref, f32[1024,128]{1,0:T(8,128)S(1)} %get-tuple-element.31.peak_ref, ...), custom_call_target="tpu_custom_call" | custom-call | tf_op jit(solution)/shard_map/last_stage/pallas_call | solution.py:391
  43.2 4.4 %all-to-all-start.1 = ((s16[16,72,128]{2,1,0:T(8,128)(2,1)}), s16[16,72,128]{2,1,0:T(8,128)(2,1)S(1)}, u32[]{:S(2)}, u32[]{:S(2)}) async-start(s16[16,72,128]{2,1,0:T(8,128)(2,1)} %last_stage.1), calls=%async_computation.1 | async-start | bytes 589824 | tf_op jit(solution)/shard_map/all_to_all | solution.py:497
  47.7 6.2 %suffix_part.1 = (f32[8,64,128]{2,1,0:T(8,128)S(1)}, f32[8,1,128]{2,1,0:T(1,128)S(1)}) custom-call(s32[2]{0:T(128)S(1)} %copy-done.2, bf16[16,72,128]{2,1,0:T(8,128)(2,1)} %get-tuple-element.21.query_ref, bf16[2,1024,1024]{2,1,0:T(8,128)(2,1)} %keys_hbm.1, bf16[2,1024,1024]{2,1,0:T(8,128)(2,1)} %values_hbm.1, bf16[2,4,1024]{2,1,0:T(4,128)(2,1)S(1)} %copy-done, ...), custom_call_target="tpu_custom_call" | custom-call | tf_op jit(solution)/shard_map/suffix_part/pallas_call | solution.py:219
  53.8 4.3 %all-to-all-done.1.got_ref = s16[16,72,128]{2,1,0:T(8,128)(2,1)S(1)} async-done(((s16[16,72,128]{2,1,0:T(8,128)(2,1)}), s16[16,72,128]{2,1,0:T(8,128)(2,1)S(1)}, u32[]{:S(2)}, u32[]{:S(2)}) %all-to-all-start.1) | async-done | bytes 294944 | tf_op jit(solution)/shard_map/all_to_all | solution.py:497
  58.2 1.1 %merge.1 = bf16[2,4,8192]{2,1,0:T(4,128)(2,1)} custom-call(s16[16,72,128]{2,1,0:T(8,128)(2,1)S(1)} %all-to-all-done.1.got_ref, f32[8,64,128]{2,1,0:T(8,128)S(1)} %get-tuple-element.35.local_ref, f32[8,1,128]{2,1,0:T(1,128)S(1)} %get-tuple-element.36.local_aux_ref), custom_call_target="tpu_custom_call" | custom-call | tf_op jit(solution)/shard_map/merge/pallas_call | solution.py:442
  (5 shorter events, 0.0 us)
Async XLA Ops:
  2.6 18.5 %all-to-all-start = ((bf16[16,72,128]{2,1,0:T(8,128)(2,1)}), bf16[16,72,128]{2,1,0:T(8,128)(2,1)S(1)}, u32[]{:S(2)}, u32[]{:S(2)}) async-start(bf16[16,72,128]{2,1,0:T(8,128)(2,1)} %get-tuple-element.21.query_ref), calls=%async_computation | async-start | bytes 589824 | tf_op jit(solution)/shard_map/all_to_all | solution.py:480
  12.1 9.1 %collective-permute-start.2 = (bf16[2,2,256,128]{3,2,1,0:T(8,128)(2,1)}, bf16[2,2,256,128]{3,2,1,0:T(8,128)(2,1)S(1)}, u32[]{:S(2)}, u32[]{:S(2)}) collective-permute-start(bf16[2,2,256,128]{3,2,1,0:T(8,128)(2,1)} %get-tuple-element.24), channel_id=1, source_target_pairs={{0,1},{1,0},{2,3},{3,2},{4,5},{5,4},{6,7},{7,6},{8,9},{9,8},{10,11... | collective-permute-start | bytes 786440 | tf_op jit(solution)/shard_map/ppermute | solution.py:471
  12.6 11.8 %collective-permute-start.1 = (bf16[2,2,256,128]{3,2,1,0:T(8,128)(2,1)S(1)}, bf16[2,2,256,128]{3,2,1,0:T(8,128)(2,1)S(1)}, u32[]{:S(2)}, u32[]{:S(2)}) collective-permute-start(bf16[2,2,256,128]{3,2,1,0:T(8,128)(2,1)S(1)} %get-tuple-element.23), channel_id=1, source_target_pairs={{0,7},{1,6},{2,5},{3,4},{4,3},{5,2},{6,1},{7,0},{8,15},{9,14},{10,... | collective-permute-start | bytes 786440 | tf_op jit(solution)/shard_map/ppermute | solution.py:471
  15.1 20.1 %collective-permute-start.3 = (bf16[2,2,256,128]{3,2,1,0:T(8,128)(2,1)S(1)}, bf16[2,2,256,128]{3,2,1,0:T(8,128)(2,1)S(1)}, u32[]{:S(2)}, u32[]{:S(2)}) collective-permute-start(bf16[2,2,256,128]{3,2,1,0:T(8,128)(2,1)S(1)} %get-tuple-element.25), channel_id=1, source_target_pairs={{0,2},{1,3},{2,0},{3,1},{4,6},{5,7},{6,4},{7,5},{8,10},{9,11},{10,... | collective-permute-start | bytes 786440 | tf_op jit(solution)/shard_map/ppermute | solution.py:471
  16.7 30.9 %copy-start = (bf16[2,4,1024]{2,1,0:T(4,128)(2,1)S(1)}, bf16[2,4,1024]{2,1,0:T(4,128)(2,1)}, u32[]{:S(2)}) copy-start(bf16[2,4,1024]{2,1,0:T(4,128)(2,1)} %new_keys_ref.1) | copy-start | bytes 49156
  16.7 30.9 %copy-start.1 = (bf16[2,4,1024]{2,1,0:T(4,128)(2,1)S(1)}, bf16[2,4,1024]{2,1,0:T(4,128)(2,1)}, u32[]{:S(2)}) copy-start(bf16[2,4,1024]{2,1,0:T(4,128)(2,1)} %new_values_ref.1) | copy-start | bytes 49156
  16.7 30.9 %copy-start.2 = (s32[2]{0:T(128)S(1)}, s32[2]{0:T(128)}, u32[]{:S(2)}) copy-start(s32[2]{0:T(128)} %len_ref.1) | copy-start | bytes 28
  16.7 18.5 %collective-permute-start = (bf16[2,2,256,128]{3,2,1,0:T(8,128)(2,1)S(1)}, bf16[2,2,256,128]{3,2,1,0:T(8,128)(2,1)S(1)}, u32[]{:S(2)}, u32[]{:S(2)}) collective-permute-start(bf16[2,2,256,128]{3,2,1,0:T(8,128)(2,1)S(1)} %head_slices.4), channel_id=1, source_target_pairs={{0,6},{1,7},{2,4},{3,5},{4,2},{5,3},{6,0},{7,1},{8,14},{9,15},{10,... | collective-permute-start | bytes 786440 | tf_op jit(solution)/shard_map/ppermute | solution.py:471
  19.3 19.0 %collective-permute-start.4 = (bf16[2,2,256,128]{3,2,1,0:T(8,128)(2,1)S(1)}, bf16[2,2,256,128]{3,2,1,0:T(8,128)(2,1)S(1)}, u32[]{:S(2)}, u32[]{:S(2)}) collective-permute-start(bf16[2,2,256,128]{3,2,1,0:T(8,128)(2,1)S(1)} %head_slices.5), channel_id=1, source_target_pairs={{0,4},{1,5},{2,6},{3,7},{4,0},{5,1},{6,2},{7,3},{8,12},{9,13},{10,... | collective-permute-start | bytes 786440 | tf_op jit(solution)/shard_map/ppermute | solution.py:471
  21.3 19.1 %collective-permute-start.5 = (bf16[2,2,256,128]{3,2,1,0:T(8,128)(2,1)S(1)}, bf16[2,2,256,128]{3,2,1,0:T(8,128)(2,1)S(1)}, u32[]{:S(2)}, u32[]{:S(2)}) collective-permute-start(bf16[2,2,256,128]{3,2,1,0:T(8,128)(2,1)S(1)} %get-tuple-element.33), channel_id=1, source_target_pairs={{0,5},{1,4},{2,7},{3,6},{4,1},{5,0},{6,3},{7,2},{8,13},{9,12},{10,... | collective-permute-start | bytes 786440 | tf_op jit(solution)/shard_map/ppermute | solution.py:471
  24.4 16.0 %collective-permute-start.6 = (bf16[2,2,256,128]{3,2,1,0:T(8,128)(2,1)S(1)}, bf16[2,2,256,128]{3,2,1,0:T(8,128)(2,1)S(1)}, u32[]{:S(2)}, u32[]{:S(2)}) collective-permute-start(bf16[2,2,256,128]{3,2,1,0:T(8,128)(2,1)S(1)} %get-tuple-element.34), channel_id=1, source_target_pairs={{0,3},{1,2},{2,1},{3,0},{4,7},{5,6},{6,5},{7,4},{8,11},{9,10},{10,... | collective-permute-start | bytes 786440 | tf_op jit(solution)/shard_map/ppermute | solution.py:471
  43.2 15.0 %all-to-all-start.1 = ((s16[16,72,128]{2,1,0:T(8,128)(2,1)}), s16[16,72,128]{2,1,0:T(8,128)(2,1)S(1)}, u32[]{:S(2)}, u32[]{:S(2)}) async-start(s16[16,72,128]{2,1,0:T(8,128)(2,1)} %last_stage.1), calls=%async_computation.1 | async-start | bytes 589824 | tf_op jit(solution)/shard_map/all_to_all | solution.py:497
